TPU v7x, 32 devices: a whole 2x2x4 slice. The times are simulated.
32 devices in a mesh: gx: 16 (over z, x, core), gy: 2 (over y).
Axes of the slice: x: 2, y: 2, z: 4, core: 2. Of those that a mesh axis runs over, the one named last changes fastest.
Arguments:
- volume_field: float32 [3, 256, 32, 128], P(None, 'gx', 'gy'), may hold values from -6 to 6
- diag_blocks: float32 [3, 3, 256, 32, 128], P(None, None, 'gx', 'gy'), may hold values from -4 to 4
- face_weights: float32 [6, 2, 256, 32, 128], P(None, None, 'gx', 'gy'), may hold values from 0.3 to 3
- boundary_field: float32 [16, 2, 1536], P('gx', 'gy'), may hold values from -6 to 6
- self_term: float32 [16, 2, 1536], P('gx', 'gy'), may hold values from 0.5 to 2
- coupling: float32 [16, 2, 1536], P('gx', 'gy'), may hold values from 0.3 to 3
- owner_map: int32 [16, 2, 1536], P('gx', 'gy'), may hold values from 0 to 1535, as said below
- left_basis: bfloat16 [32, 16, 2, 1536], P('gy', 'gx'), may hold values from -1 to 1
- right_basis: bfloat16 [256, 16, 2, 1536], P('gx', None, 'gy'), may hold values from -0.0390625 to 0.0390625
Outputs:
- volume_out: float32 [3, 256, 32, 128], P(None, 'gx', 'gy')
- boundary_out: float32 [16, 2, 1536], P('gx', 'gy')
Inputs may be any that keep to these rules, and one draw needn't show every extreme that they name: `owner_map`: within each subdomain (p, q) the 1536 entries name every surface edge of that subdomain exactly once.
All inputs are finite; a program needn't handle non-finite values.
Results may differ from a plain program's by a relative error of at most 0.0017.
Values may be sent and summed in bfloat16 or wider, within the bound.
No kernel may reach another device: no remote copies, remote signals or barrier semaphores. Data moves between devices by JAX's collectives and lax.ppermute only.
A program may use at most 64 MiB of HBM per device.

v0:
```python
import jax
import jax.numpy as jnp
from jax import lax
from jax.sharding import PartitionSpec as P


def with_halo(value, sides, width):
    for axis, dim in sides:
        devices, length = (lax.axis_size(axis), value.shape[dim])
        up = [(i, (i + 1) % devices) for i in range(devices - 1)]
        down = [(j, i) for i, j in up]
        last = lax.slice_in_dim(value, length - width, length, axis=dim)
        initial = lax.slice_in_dim(value, 0, width, axis=dim)
        before = lax.ppermute(last, axis, up)
        after = lax.ppermute(initial, axis, down)
        value = jnp.concatenate([before, value, after], axis=dim)
    return value


def apply_blocks(field_in, diag_blocks, face_weights, neighbours):
    comp_rows = []
    for comp in range(3):
        accum_row = (
            diag_blocks[comp, 0] * field_in[0]
            + diag_blocks[comp, 1] * field_in[1]
            + diag_blocks[comp, 2] * field_in[2]
        )
        comp_rows.append(accum_row)
    for offset in range(6):
        direction = offset // 2
        tangent = [comp for comp in range(3) if comp != direction]
        for slot in range(2):
            comp_rows[tangent[slot]] = (
                comp_rows[tangent[slot]] - face_weights[offset, slot] * neighbours[offset][slot]
            )
    return jnp.stack(comp_rows)


def on_device(
    volume_field,
    diag_blocks,
    face_weights,
    boundary_field,
    self_term,
    coupling,
    owner_map,
    left_basis,
    right_basis,
):
    z_padded = jnp.pad(volume_field[0:2], ((0, 0), (0, 0), (0, 0), (1, 1)))
    plus_z = z_padded[..., 2:]
    minus_z = z_padded[..., :-2]
    padded = with_halo(volume_field, (("gx", 1), ("gy", 2)), 1)
    plus_x = padded[1:3, 2:, 1:-1]
    minus_x = padded[1:3, :-2, 1:-1]
    plus_y = padded[0::2, 1:-1, 2:]
    minus_y = padded[0::2, 1:-1, :-2]
    neighbours = [plus_x, minus_x, plus_y, minus_y, plus_z, minus_z]
    stiffness = apply_blocks(volume_field, diag_blocks, face_weights, neighbours)
    cells_x = volume_field.shape[1]
    cells_y = volume_field.shape[2]
    boundary_count = boundary_field.shape[2]
    surface = jnp.stack([volume_field[..., 0], volume_field[..., -1]]).reshape(boundary_count)
    owner_flat = owner_map.reshape(boundary_count)
    edge_trace = surface[owner_flat].reshape(boundary_field.shape)
    placed = (
        jnp.zeros((boundary_count,), jnp.float32)
        .at[owner_flat]
        .set((coupling * boundary_field).reshape(boundary_count))
    )
    placed = placed.reshape(2, 3, cells_x, cells_y)
    volume_out = stiffness.at[:, :, :, 0].add(placed[0]).at[:, :, :, -1].add(placed[1])
    boundary_half = boundary_field.astype(jnp.bfloat16)
    gathered = lax.all_gather(boundary_half, "gx", axis=0, tiled=True)
    coef = jnp.einsum("rxbk,xbk->r", right_basis, gathered, preferred_element_type=jnp.float32)
    coef_half = coef.astype(jnp.bfloat16)
    partial_value = jnp.einsum(
        "rabk,r->abk", left_basis, coef_half, preferred_element_type=jnp.float32
    )
    integral = lax.psum_scatter(partial_value, "gy", scatter_dimension=1, tiled=True)
    boundary_out = self_term * boundary_field + integral + coupling * edge_trace
    return (volume_out, boundary_out)


def solution(mesh):
    return jax.shard_map(
        on_device,
        mesh=mesh,
        in_specs=(
            P(None, "gx", "gy", None),
            P(None, None, "gx", "gy", None),
            P(None, None, "gx", "gy", None),
            P("gx", "gy", None),
            P("gx", "gy", None),
            P("gx", "gy", None),
            P("gx", "gy", None),
            P("gy", "gx", None, None),
            P("gx", None, "gy", None),
        ),
        out_specs=(P(None, "gx", "gy", None), P("gx", "gy", None)),
        check_vma=False,
    )
```

profile of v0, /device:TPU:0, one launch (start us, length us, event | category | flops | bytes accessed | tf_op | source)
XLA Modules:
  0.0 75.5 jit_solution(9150187020478586098)
XLA Ops:
  0.6 0.0 copy-start
  0.6 0.0 copy-start.5
  0.7 0.0 copy-start.4
  0.7 0.0 copy-start.8
  0.7 1.4 %fusion.40 = (f32[3,1,16,128]{3,2,1,0:T(8,128)}, f32[3,1,16,128]{3,2,1,0:T(8,128)}) fusion(f32[3,16,16,128]{3,2,1,0:T(8,128)} %param.13), kind=kLoop, calls=%fused_computation.77 | loop fusion | bytes 98304 | tf_op jit(solution)/shard_map/slice | solution.py:13
  2.1 3.0 %collective-permute-start = (f32[3,1,16,128]{3,2,1,0:T(8,128)}, f32[3,1,16,128]{3,2,1,0:T(8,128)}, u32[]{:S(2)}, u32[]{:S(2)}) collective-permute-start(f32[3,1,16,128]{3,2,1,0:T(8,128)} %get-tuple-element.42), channel_id=1, source_target_pairs={{0,2},{2,4},{4,6},{6,8},{8,10},{10,12},{12,14},{14,16},{16,18},{18... | collective-permute-start | bytes 73736 | tf_op jit(solution)/shard_map/ppermute | solution.py:14
  5.1 1.3 %collective-permute-start.1 = (f32[3,1,16,128]{3,2,1,0:T(8,128)}, f32[3,1,16,128]{3,2,1,0:T(8,128)}, u32[]{:S(2)}, u32[]{:S(2)}) collective-permute-start(f32[3,1,16,128]{3,2,1,0:T(8,128)} %get-tuple-element.41), channel_id=1, source_target_pairs={{2,0},{4,2},{6,4},{8,6},{10,8},{12,10},{14,12},{16,14},{18,16},{20... | collective-permute-start | bytes 73736 | tf_op jit(solution)/shard_map/ppermute | solution.py:15
  6.4 1.3 %fusion.39 = (f32[3,16,16,1]{3,2,1,0:T(8,128)S(1)}, f32[3,16,16,1]{3,2,1,0:T(8,128)S(1)}) fusion(f32[3,16,16,128]{3,2,1,0:T(8,128)} %param.13), kind=kLoop, calls=%fused_computation.76 | loop fusion | bytes 12288 | tf_op jit(solution)/shard_map/slice | solution.py:63
  7.7 0.3 copy.61
  8.0 0.4 copy.62
  8.4 0.1 reshape.175
  8.5 0.0 copy-done.5
  8.6 0.0 copy-done.4
  8.6 24.6 %all_gather.3 = bf16[16,1,1536]{2,1,0:T(2,128)(2,1)S(1)} all-gather(bf16[1,1,1536]{2,1,0:T(2,128)(2,1)S(1)} %convert_element_type.8), channel_id=1, replica_groups=mesh['gx'=16,'gy'=2] {'gx'}, dimensions={0}, use_global_device_ids=true | all-gather | bytes 52224 | tf_op jit(solution)/shard_map/all_gather | solution.py:74
  33.2 0.0 copy-done
  33.2 0.0 copy-done.8
  33.2 1.1 %fusion.4 = f32[1,2,1536]{2,0,1:T(1,128)S(1)} fusion(bf16[16,16,1536]{2,1,0:T(8,128)(2,1)S(1)} %bitcast.103, bf16[16,1,1536]{2,1,0:T(2,128)(2,1)S(1)} %all_gather.3, bf16[16,2,1536]{2,1,0:T(2,128)(2,1)S(1)} %bitcast.100), kind=kOutput, calls=%fused_computation.10 | convolution fusion | flops 884752 | bytes 946176 | tf_op jit(solution)/shard_map/rabk,r->abk/dot_general | solution.py:77
  34.4 8.1 %all-reduce.1 = f32[1,2,1536]{2,1,0:T(2,128)S(1)} all-reduce(f32[1,2,1536]{2,1,0:T(2,128)S(1)} %copy.58), channel_id=2, replica_groups=mesh['gx'=16,'gy'=2] {'gy'}, use_global_device_ids=true, to_apply=%region_1.2.clone | all-reduce | flops 3072 | bytes 24576
  42.5 0.0 copy-start.1
  42.5 0.0 copy-start.3
  42.5 8.4 %gather_fusion = f32[1536]{0:T(1024)S(1)} fusion(f32[1536]{0:T(1024)S(1)} %reshape.175, s32[2048]{0:T(1024)S(1)} %pad_clamp_fusion), kind=kCustom, calls=%fused_computation | custom fusion | bytes 18432 | tf_op jit(solution)/shard_map/gather | solution.py:65
  50.9 0.0 copy-start.2
  50.9 0.0 copy-done.9
  50.9 0.7 dynamic-slice.14
  51.6 0.0 copy-done.6
  51.6 0.0 copy-done.7
  51.6 1.3 %fusion.34 = (f32[1,1,1536]{2,1,0:T(1,128)}, f32[1536]{0:T(1024)S(1)}) fusion(f32[1,2,1536]{2,1,0:T(2,128)S(1)} %all-reduce.1, u32[]{:T(128)} %bitcast.32, f32[1,1,1536]{2,1,0:T(1,128)S(1)} %copy-done.6, f32[1536]{0:T(1024)S(1)} %gather_fusion, f32[1,1,1536]{2,1,0:T(1,128)S(1)} %copy-done.7, f32[1,1,1536]{2,1,0:T(1,128)S(1)} %copy-done.4), kind=kLoop, calls=%fused_computation.70 | loop fusion | flops 7680 | bytes 43012 | tf_op jit(solution)/shard_map/add | solution.py:81
  52.9 6.2 %scatter_custom_fusion = f32[1536]{0:T(1024)S(1)} fusion(s32[1536]{0:T(1024)S(1)} %fusion.33, f32[1536]{0:T(1024)S(1)} %get-tuple-element.48, f32[]{:T(128)} %constant.58.clone.1), kind=kCustom, calls=%fused_computation.72 | custom fusion | bytes 6148 | tf_op jit(solution)/shard_map/scatter | solution.py:69
  59.1 0.6 fusion.41
  59.7 0.0 copy-done.1
  59.7 0.1 reshape.170
  59.8 0.8 reshape.171
  60.5 0.0 collective-permute-done
  60.5 0.7 constant_dynamic-update-slice_fusion.6
  61.3 0.1 constant_dynamic-update-slice_fusion.4
  61.4 0.0 collective-permute-done.1
  61.4 0.7 constant_dynamic-update-slice_fusion.3
  62.2 2.4 %collective-permute-start.2 = (f32[3,18,1,128]{3,2,1,0:T(1,128)S(1)}, f32[3,18,1,128]{3,2,1,0:T(1,128)S(1)}, u32[]{:S(2)}, u32[]{:S(2)}) collective-permute-start(f32[3,18,1,128]{3,2,1,0:T(1,128)S(1)} %get-tuple-element.34), channel_id=1, source_target_pairs={{0,1},{2,3},{4,5},{6,7},{8,9},{10,11},{12,13},{14,15},{16,17},{18,... | collective-permute-start | bytes 82952 | tf_op jit(solution)/shard_map/ppermute | solution.py:14
  64.6 1.3 %collective-permute-start.3 = (f32[3,18,1,128]{3,2,1,0:T(1,128)S(1)}, f32[3,18,1,128]{3,2,1,0:T(1,128)S(1)}, u32[]{:S(2)}, u32[]{:S(2)}) collective-permute-start(f32[3,18,1,128]{3,2,1,0:T(1,128)S(1)} %get-tuple-element.35), channel_id=1, source_target_pairs={{1,0},{3,2},{5,4},{7,6},{9,8},{11,10},{13,12},{15,14},{17,16},{19,... | collective-permute-start | bytes 82952 | tf_op jit(solution)/shard_map/ppermute | solution.py:15
  65.9 0.2 fusion.12
  66.1 0.0 collective-permute-done.2
  66.1 4.2 %collective-permute-done.3 = f32[3,18,1,128]{3,2,1,0:T(1,128)S(1)} collective-permute-done((f32[3,18,1,128]{3,2,1,0:T(1,128)S(1)}, f32[3,18,1,128]{3,2,1,0:T(1,128)S(1)}, u32[]{:S(2)}, u32[]{:S(2)}) %collective-permute-start.3) | collective-permute-done | bytes 27680 | tf_op jit(solution)/shard_map/ppermute | solution.py:15
  70.4 0.1 pad_maximum_fusion
  70.5 0.2 fusion.8
  70.7 0.1 fusion.14
  70.8 0.8 %pad_maximum_fusion.1 = f32[3,16,16,128]{3,2,1,0:T(8,128)} fusion(f32[1,16,16,128]{3,2,1,0:T(8,128)S(1)} %fusion.14, f32[1,16,16,128]{3,2,1,0:T(8,128)S(1)} %fusion.12, f32[1,16,16,128]{3,2,1,0:T(8,128)S(1)} %fusion.8), kind=kLoop, calls=%fused_computation.12 | loop fusion | flops 196608 | bytes 786432 | tf_op jit(solution)/shard_map/stack | solution.py:36
  71.6 2.1 %copy.51 = f32[3,16,16,128]{2,1,0,3:T(8,128)S(1)} copy(f32[3,16,16,128]{3,2,1,0:T(8,128)} %pad_maximum_fusion.1) | data formatting | bytes 786432 | tf_op jit(solution)/shard_map/stack | solution.py:36
  73.7 1.8 %copy.54 = f32[3,16,16,128]{3,2,1,0:T(8,128)} copy(f32[3,16,16,128]{2,1,0,3:T(8,128)S(1)} %fusion.31) | data formatting | bytes 786432
  (15 shorter events, 0.2 us)
Async XLA Ops:
  0.6 32.6 %copy-start = (bf16[16,1,2,1536]{3,2,1,0:T(2,128)(2,1)S(1)}, bf16[16,1,2,1536]{3,2,1,0:T(2,128)(2,1)}, u32[]{:S(2)}) copy-start(bf16[16,1,2,1536]{3,2,1,0:T(2,128)(2,1)} %param.20) | copy-start | bytes 294916
  0.6 7.9 %copy-start.5 = (s32[1,1,1536]{2,1,0:T(1,128)S(1)}, s32[1,1,1536]{2,1,0:T(1,128)}, u32[]{:S(2)}) copy-start(s32[1,1,1536]{2,1,0:T(1,128)} %param.19) | copy-start | bytes 18436
  0.7 7.9 %copy-start.4 = (f32[1,1,1536]{2,1,0:T(1,128)S(1)}, f32[1,1,1536]{2,1,0:T(1,128)}, u32[]{:S(2)}) copy-start(f32[1,1,1536]{2,1,0:T(1,128)} %param.16) | copy-start | bytes 18436
  0.7 32.6 %copy-start.8 = (bf16[16,16,1,1536]{3,1,2,0:T(8,128)(2,1)S(1)}, bf16[16,16,1,1536]{3,1,2,0:T(8,128)(2,1)}, u32[]{:S(2)}) copy-start(bf16[16,16,1,1536]{3,1,2,0:T(8,128)(2,1)} %param.21) | copy-start | bytes 2359300
  2.1 58.4 %collective-permute-start = (f32[3,1,16,128]{3,2,1,0:T(8,128)}, f32[3,1,16,128]{3,2,1,0:T(8,128)}, u32[]{:S(2)}, u32[]{:S(2)}) collective-permute-start(f32[3,1,16,128]{3,2,1,0:T(8,128)} %get-tuple-element.42), channel_id=1, source_target_pairs={{0,2},{2,4},{4,6},{6,8},{8,10},{10,12},{12,14},{14,16},{16,18},{18... | collective-permute-start | bytes 73736 | tf_op jit(solution)/shard_map/ppermute | solution.py:14
  5.1 56.3 %collective-permute-start.1 = (f32[3,1,16,128]{3,2,1,0:T(8,128)}, f32[3,1,16,128]{3,2,1,0:T(8,128)}, u32[]{:S(2)}, u32[]{:S(2)}) collective-permute-start(f32[3,1,16,128]{3,2,1,0:T(8,128)} %get-tuple-element.41), channel_id=1, source_target_pairs={{2,0},{4,2},{6,4},{8,6},{10,8},{12,10},{14,12},{16,14},{18,16},{20... | collective-permute-start | bytes 73736 | tf_op jit(solution)/shard_map/ppermute | solution.py:15
  42.5 8.5 %copy-start.9 = (u32[32]{0:T(128)S(1)}, u32[32]{0:T(128)}, u32[]{:S(2)}) copy-start(u32[32]{0:T(128)} %constant.72) | copy-start | bytes 388
  42.5 9.1 %copy-start.6 = (f32[1,1,1536]{2,1,0:T(1,128)S(1)}, f32[1,1,1536]{2,1,0:T(1,128)}, u32[]{:S(2)}) copy-start(f32[1,1,1536]{2,1,0:T(1,128)} %param.18) | copy-start | bytes 18436
  42.5 9.1 %copy-start.7 = (f32[1,1,1536]{2,1,0:T(1,128)S(1)}, f32[1,1,1536]{2,1,0:T(1,128)}, u32[]{:S(2)}) copy-start(f32[1,1,1536]{2,1,0:T(1,128)} %param.17) | copy-start | bytes 18436
  42.5 17.2 %copy-start.1 = (f32[3,16,16,128]{3,2,1,0:T(8,128)S(1)}, f32[3,16,16,128]{3,2,1,0:T(8,128)}, u32[]{:S(2)}) copy-start(f32[3,16,16,128]{3,2,1,0:T(8,128)} %param.13) | copy-start | bytes 1179652
  42.5 23.4 %copy-start.3 = (f32[3,3,16,16,128]{4,3,2,1,0:T(8,128)S(1)}, f32[3,3,16,16,128]{4,3,2,1,0:T(8,128)}, u32[]{:S(2)}) copy-start(f32[3,3,16,16,128]{4,3,2,1,0:T(8,128)} %param.14) | copy-start | bytes 3538948
  50.9 15.0 %copy-start.2 = (f32[6,2,16,16,128]{4,3,2,1,0:T(8,128)S(1)}, f32[6,2,16,16,128]{4,3,2,1,0:T(8,128)}, u32[]{:S(2)}) copy-start(f32[6,2,16,16,128]{4,3,2,1,0:T(8,128)} %param.15) | copy-start | bytes 4718596
  62.2 4.0 %collective-permute-start.2 = (f32[3,18,1,128]{3,2,1,0:T(1,128)S(1)}, f32[3,18,1,128]{3,2,1,0:T(1,128)S(1)}, u32[]{:S(2)}, u32[]{:S(2)}) collective-permute-start(f32[3,18,1,128]{3,2,1,0:T(1,128)S(1)} %get-tuple-element.34), channel_id=1, source_target_pairs={{0,1},{2,3},{4,5},{6,7},{8,9},{10,11},{12,13},{14,15},{16,17},{18,... | collective-permute-start | bytes 82952 | tf_op jit(solution)/shard_map/ppermute | solution.py:14
  64.6 5.8 %collective-permute-start.3 = (f32[3,18,1,128]{3,2,1,0:T(1,128)S(1)}, f32[3,18,1,128]{3,2,1,0:T(1,128)S(1)}, u32[]{:S(2)}, u32[]{:S(2)}) collective-permute-start(f32[3,18,1,128]{3,2,1,0:T(1,128)S(1)} %get-tuple-element.35), channel_id=1, source_target_pairs={{1,0},{3,2},{5,4},{7,6},{9,8},{11,10},{13,12},{15,14},{17,16},{19,... | collective-permute-start | bytes 82952 | tf_op jit(solution)/shard_map/ppermute | solution.py:15
where the time goes:
time: 75.9 us; the launch traced here: 75.5 us
  blocking collectives  32.7 us (43%)
  local copies, waits for them, and re-layouts  25.7 us (34%)
  starting transfers between devices  7.98 us (11%)
  waiting for transfers between devices  4.27 us (6%)
  other arithmetic  2.72 us (4%)
  matrix products  1.12 us (1%)
  between operations  0.9 us (1%)
    all_gather x1, blocking collectives, on_device(): gathered = lax.all_gather(boundary_half, 'gx', axis=0, tiled=True)  24.6 us
    gather x1, local copies, waits for them, and re-layouts, on_device(): edge_trace = surface[owner_flat].reshape(boundary_field.shape)  8.39 us
    unnamed x1, blocking collectives  8.11 us
    scatter x1, local copies, waits for them, and re-layouts, on_device(): placed = jnp.zeros((boundary_count,), jnp.float32).at[owner_flat].set((co...  6.18 us
    ppermute x2, starting transfers between devices, with_halo(): before = lax.ppermute(last, axis, up)  5.41 us
    ppermute x2, waiting for transfers between devices, with_halo(): after = lax.ppermute(initial, axis, down)  4.23 us
    unnamed x26, local copies, waits for them, and re-layouts  4.02 us
    ppermute x2, starting transfers between devices, with_halo(): after = lax.ppermute(initial, axis, down)  2.57 us
  transfers between devices with their start and end apart: 4, of which 1 were waited for; matrix products, arithmetic and copies ran while one was open for 29% of the time, Pallas kernels for 0%

commit v1 on v0

--- a/solution.py
+++ b/solution.py
@@ -2,6 +2,18 @@
 import jax.numpy as jnp
 from jax import lax
 from jax.sharding import PartitionSpec as P
+
+
+def product_in_turn(x, axis, dim, term):
+    size, index = (lax.axis_size(axis), lax.axis_index(axis))
+    left = [(i, (i - 1) % size) for i in range(size)]
+    rows = x.shape[dim]
+    block = x
+    total = term(block, index * rows)
+    for step in range(1, size):
+        block = lax.ppermute(block, axis, left)
+        total = total + term(block, (index + step) % size * rows)
+    return total
 
 
 def with_halo(value, sides, width):
@@ -71,8 +83,17 @@
     placed = placed.reshape(2, 3, cells_x, cells_y)
     volume_out = stiffness.at[:, :, :, 0].add(placed[0]).at[:, :, :, -1].add(placed[1])
     boundary_half = boundary_field.astype(jnp.bfloat16)
-    gathered = lax.all_gather(boundary_half, "gx", axis=0, tiled=True)
-    coef = jnp.einsum("rxbk,xbk->r", right_basis, gathered, preferred_element_type=jnp.float32)
+    coef = product_in_turn(
+        boundary_half,
+        "gx",
+        0,
+        lambda part, at: jnp.einsum(
+            "rxbk,xbk->r",
+            lax.dynamic_slice_in_dim(right_basis, at, part.shape[0], axis=1),
+            part,
+            preferred_element_type=jnp.float32,
+        ),
+    )
     coef_half = coef.astype(jnp.bfloat16)
     partial_value = jnp.einsum(
         "rabk,r->abk", left_basis, coef_half, preferred_element_type=jnp.float32

time: 75.9 us -> 139 us (1.83)
  starting transfers between devices: 7.98 us -> 69 us
  blocking collectives: 32.7 us -> 9.8 us
  matrix products: 1.12 us -> 9.3 us
  waiting for transfers between devices: 4.27 us -> 10.7 us
  local copies, waits for them, and re-layouts: 25.7 us -> 31.6 us
  other arithmetic: 2.72 us -> 6.75 us
    ppermute x0 -> x15, starting transfers between devices: none -> 60.5 us  [product_in_turn(): block = lax.ppermute(block, axis, left)]
    all_gather x1 -> x0, blocking collectives: 24.6 us -> none  [on_device(): gathered = lax.all_gather(boundary_half, 'gx', axis=0, tiled=True)]
    ppermute x0 -> x15, waiting for transfers between devices: none -> 10.7 us  [product_in_turn(): block = lax.ppermute(block, axis, left)]
    dot_general x0 -> x15, matrix products: none -> 8.15 us  [on_device(): jnp.einsum('rxbk,xbk->r', lax.dynamic_slice_in_dim(right_basis, at, part....]
    ppermute x2, waiting for transfers between devices: 4.23 us -> 0.01 us  [with_halo(): after = lax.ppermute(initial, axis, down)]
    dynamic_slice x0 -> x1, local copies, waits for them, and re-layouts: none -> 2.7 us  [on_device(): lax.dynamic_slice_in_dim(right_basis, at, part.shape[0], axis=1)]
    slice x1, local copies, waits for them, and re-layouts: 0.04 us -> 1.85 us  [with_halo(): last = lax.slice_in_dim(value, length - width, length, axis=dim)]
    unnamed x1, blocking collectives: 8.11 us -> 9.8 us
  transfers between devices with their start and end apart: 4 -> 19, of which waited for: 1 -> 13; matrix products, arithmetic and copies ran while one was open for 29% -> 29% of each run, Pallas kernels for 0% -> 0%
where the time goes in v1:
time: 139 us; the launch traced here: 138 us
  starting transfers between devices  69 us (50%)
  local copies, waits for them, and re-layouts  31.6 us (23%)
  waiting for transfers between devices  10.7 us (8%)
  blocking collectives  9.8 us (7%)
  matrix products  9.3 us (7%)
  other arithmetic  6.75 us (5%)
    ppermute x15, starting transfers between devices, product_in_turn(): block = lax.ppermute(block, axis, left)  60.5 us
    ppermute x15, waiting for transfers between devices, product_in_turn(): block = lax.ppermute(block, axis, left)  10.7 us
    unnamed x1, blocking collectives  9.8 us
    gather x1, local copies, waits for them, and re-layouts, on_device(): edge_trace = surface[owner_flat].reshape(boundary_field.shape)  8.39 us
    dot_general x15, matrix products, on_device(): jnp.einsum('rxbk,xbk->r', lax.dynamic_slice_in_dim(right_basis, at, part....  8.15 us
    scatter x1, local copies, waits for them, and re-layouts, on_device(): placed = jnp.zeros((boundary_count,), jnp.float32).at[owner_flat].set((co...  6.18 us
    ppermute x2, starting transfers between devices, with_halo(): before = lax.ppermute(last, axis, up)  5.91 us
    unnamed x46, local copies, waits for them, and re-layouts  5.31 us
  transfers between devices with their start and end apart: 19, of which 13 were waited for; matrix products, arithmetic and copies ran while one was open for 29% of the time, Pallas kernels for 0%

profile of v1, /device:TPU:0, one launch (start us, length us, event | category | flops | bytes accessed | tf_op | source)
XLA Modules:
  0.0 138.4 jit_solution(5151179981781235638)
XLA Ops:
  1.4 5.4 %collective-permute-start.4 = (bf16[1,1,1536]{2,1,0:T(2,128)(2,1)S(1)}, bf16[1,1,1536]{2,1,0:T(2,128)(2,1)}, u32[]{:S(2)}, u32[]{:S(2)}) collective-permute-start(bf16[1,1,1536]{2,1,0:T(2,128)(2,1)S(1)} %convert_element_type.8), channel_id=1, source_target_pairs={{0,30},{2,0},{4,2},{6,4},{8,6},{10,8},{12,10},{14,12},{16,14},{18,... | collective-permute-start | bytes 9224 | tf_op jit(solution)/shard_map/ppermute | solution.py:14
  6.9 1.4 fusion.68
  8.3 1.9 %collective-permute-start = (f32[3,1,16,128]{3,2,1,0:T(8,128)}, f32[3,1,16,128]{3,2,1,0:T(8,128)}, u32[]{:S(2)}, u32[]{:S(2)}) collective-permute-start(f32[3,1,16,128]{3,2,1,0:T(8,128)} %get-tuple-element.56), channel_id=1, source_target_pairs={{0,2},{2,4},{4,6},{6,8},{8,10},{10,12},{12,14},{14,16},{16,18},{18... | collective-permute-start | bytes 73736 | tf_op jit(solution)/shard_map/ppermute | solution.py:26
  10.2 1.3 collective-permute-start.1
  11.6 1.3 fusion.67
  13.0 2.7 %constant_dynamic-slice_fusion = (bf16[16,1,1,1536]{3,1,2,0:T(2,128)(2,1)}, bf16[16,1,1,1536]{3,1,2,0:T(2,128)(2,1)}, bf16[16,1,1,1536]{3,1,2,0:T(2,128)(2,1)}, ...) fusion(bf16[16,16,1,1536]{3,1,2,0:T(8,128)(2,1)S(1)} %copy-done, ...), kind=kLoop, calls=%fused_computation.132 | loop fusion | bytes 1572928 | tf_op jit(solution)/shard_map/dynamic_slice | solution.py:92
  16.8 8.4 %gather_fusion = f32[1536]{0:T(1024)S(1)} fusion(f32[1536]{0:T(1024)S(1)} %reshape.295, s32[2048]{0:T(1024)S(1)} %pad_clamp_fusion), kind=kCustom, calls=%fused_computation | custom fusion | bytes 18432 | tf_op jit(solution)/shard_map/gather | solution.py:77
  25.8 2.2 %collective-permute-start.5 = (bf16[1,1,1536]{2,1,0:T(2,128)(2,1)}, bf16[1,1,1536]{2,1,0:T(2,128)(2,1)S(1)}, u32[]{:S(2)}, u32[]{:S(2)}) collective-permute-start(bf16[1,1,1536]{2,1,0:T(2,128)(2,1)} %collective-permute-done.4), channel_id=1, source_target_pairs={{0,30},{2,0},{4,2},{6,4},{8,6},{10,8},{12,10},{14,12},{16,14},{18,... | collective-permute-start | bytes 9224 | tf_op jit(solution)/shard_map/ppermute | solution.py:14
  28.0 1.0 fusion
  29.5 4.4 %collective-permute-start.6 = (bf16[1,1,1536]{2,1,0:T(2,128)(2,1)S(1)}, bf16[1,1,1536]{2,1,0:T(2,128)(2,1)S(1)}, u32[]{:S(2)}, u32[]{:S(2)}) collective-permute-start(bf16[1,1,1536]{2,1,0:T(2,128)(2,1)S(1)} %collective-permute-done.5), channel_id=1, source_target_pairs={{0,30},{2,0},{4,2},{6,4},{8,6},{10,8},{12,10},{14,12},{16,14},{18,... | collective-permute-start | bytes 9224 | tf_op jit(solution)/shard_map/ppermute | solution.py:14
  34.0 1.0 fusion.1
  35.3 4.4 %collective-permute-start.7 = (bf16[1,1,1536]{2,1,0:T(2,128)(2,1)S(1)}, bf16[1,1,1536]{2,1,0:T(2,128)(2,1)S(1)}, u32[]{:S(2)}, u32[]{:S(2)}) collective-permute-start(bf16[1,1,1536]{2,1,0:T(2,128)(2,1)S(1)} %collective-permute-done.6), channel_id=1, source_target_pairs={{0,30},{2,0},{4,2},{6,4},{8,6},{10,8},{12,10},{14,12},{16,14},{18,... | collective-permute-start | bytes 9224 | tf_op jit(solution)/shard_map/ppermute | solution.py:14
  39.7 1.0 fusion.2
  41.1 4.4 %collective-permute-start.8 = (bf16[1,1,1536]{2,1,0:T(2,128)(2,1)S(1)}, bf16[1,1,1536]{2,1,0:T(2,128)(2,1)S(1)}, u32[]{:S(2)}, u32[]{:S(2)}) collective-permute-start(bf16[1,1,1536]{2,1,0:T(2,128)(2,1)S(1)} %collective-permute-done.7), channel_id=1, source_target_pairs={{0,30},{2,0},{4,2},{6,4},{8,6},{10,8},{12,10},{14,12},{16,14},{18,... | collective-permute-start | bytes 9224 | tf_op jit(solution)/shard_map/ppermute | solution.py:14
  45.5 1.0 fusion.3
  46.8 4.4 %collective-permute-start.9 = (bf16[1,1,1536]{2,1,0:T(2,128)(2,1)S(1)}, bf16[1,1,1536]{2,1,0:T(2,128)(2,1)S(1)}, u32[]{:S(2)}, u32[]{:S(2)}) collective-permute-start(bf16[1,1,1536]{2,1,0:T(2,128)(2,1)S(1)} %collective-permute-done.8), channel_id=1, source_target_pairs={{0,30},{2,0},{4,2},{6,4},{8,6},{10,8},{12,10},{14,12},{16,14},{18,... | collective-permute-start | bytes 9224 | tf_op jit(solution)/shard_map/ppermute | solution.py:14
  51.2 1.0 fusion.4
  52.6 4.4 %collective-permute-start.10 = (bf16[1,1,1536]{2,1,0:T(2,128)(2,1)S(1)}, bf16[1,1,1536]{2,1,0:T(2,128)(2,1)S(1)}, u32[]{:S(2)}, u32[]{:S(2)}) collective-permute-start(bf16[1,1,1536]{2,1,0:T(2,128)(2,1)S(1)} %collective-permute-done.9), channel_id=1, source_target_pairs={{0,30},{2,0},{4,2},{6,4},{8,6},{10,8},{12,10},{14,12},{16,14},{18,... | collective-permute-start | bytes 9224 | tf_op jit(solution)/shard_map/ppermute | solution.py:14
  57.0 1.0 fusion.5
  58.3 4.4 %collective-permute-start.11 = (bf16[1,1,1536]{2,1,0:T(2,128)(2,1)S(1)}, bf16[1,1,1536]{2,1,0:T(2,128)(2,1)S(1)}, u32[]{:S(2)}, u32[]{:S(2)}) collective-permute-start(bf16[1,1,1536]{2,1,0:T(2,128)(2,1)S(1)} %collective-permute-done.10), channel_id=1, source_target_pairs={{0,30},{2,0},{4,2},{6,4},{8,6},{10,8},{12,10},{14,12},{16,14},{18,... | collective-permute-start | bytes 9224 | tf_op jit(solution)/shard_map/ppermute | solution.py:14
  62.7 1.0 fusion.6
  63.7 1.4 constant_dynamic-update-slice_fusion.6
  65.1 0.8 constant_dynamic-update-slice_fusion.4
  66.0 1.6 %constant_dynamic-update-slice_fusion.3 = (f32[3,17,16,128]{3,2,1,0:T(8,128)S(1)}, f32[3,18,16,128]{3,2,1,0:T(8,128)}) fusion(f32[3,17,16,128]{3,2,1,0:T(8,128)S(1)} %get-tuple-element.52, f32[3,1,16,128]{3,2,1,0:T(8,128)} %collective-permute-done.1, f32[3,18,16,128]{3,2,1,0:T(8,128)} %get-tuple-element.53), kind=kLoop, calls=%fused_computation.107 | loop fusion | bytes 73728 | tf_op jit(solution)/shard_map/concatenate | solution.py:28
  67.5 1.8 %fusion.66 = (f32[3,18,1,128]{3,2,1,0:T(1,128)}, f32[3,18,1,128]{3,2,1,0:T(1,128)}) fusion(f32[3,18,16,128]{3,2,1,0:T(8,128)} %get-tuple-element.58), kind=kLoop, calls=%fused_computation.152 | loop fusion | bytes 110592 | tf_op jit(solution)/shard_map/slice | solution.py:24
  69.4 4.0 %collective-permute-start.2 = (f32[3,18,1,128]{3,2,1,0:T(1,128)}, f32[3,18,1,128]{3,2,1,0:T(1,128)}, u32[]{:S(2)}, u32[]{:S(2)}) collective-permute-start(f32[3,18,1,128]{3,2,1,0:T(1,128)} %get-tuple-element.48), channel_id=1, source_target_pairs={{0,1},{2,3},{4,5},{6,7},{8,9},{10,11},{12,13},{14,15},{16,17},{18,... | collective-permute-start | bytes 82952 | tf_op jit(solution)/shard_map/ppermute | solution.py:26
  73.4 1.3 collective-permute-start.3
  75.7 1.2 collective-permute-done.12
  76.9 4.4 %collective-permute-start.13 = (bf16[1,1,1536]{2,1,0:T(2,128)(2,1)S(1)}, bf16[1,1,1536]{2,1,0:T(2,128)(2,1)S(1)}, u32[]{:S(2)}, u32[]{:S(2)}) collective-permute-start(bf16[1,1,1536]{2,1,0:T(2,128)(2,1)S(1)} %collective-permute-done.12), channel_id=1, source_target_pairs={{0,30},{2,0},{4,2},{6,4},{8,6},{10,8},{12,10},{14,12},{16,14},{18,... | collective-permute-start | bytes 9224 | tf_op jit(solution)/shard_map/ppermute | solution.py:14
  81.4 1.2 collective-permute-done.13
  82.6 4.4 %collective-permute-start.14 = (bf16[1,1,1536]{2,1,0:T(2,128)(2,1)S(1)}, bf16[1,1,1536]{2,1,0:T(2,128)(2,1)S(1)}, u32[]{:S(2)}, u32[]{:S(2)}) collective-permute-start(bf16[1,1,1536]{2,1,0:T(2,128)(2,1)S(1)} %collective-permute-done.13), channel_id=1, source_target_pairs={{0,30},{2,0},{4,2},{6,4},{8,6},{10,8},{12,10},{14,12},{16,14},{18,... | collective-permute-start | bytes 9224 | tf_op jit(solution)/shard_map/ppermute | solution.py:14
  87.2 1.2 collective-permute-done.14
  88.4 4.4 %collective-permute-start.15 = (bf16[1,1,1536]{2,1,0:T(2,128)(2,1)S(1)}, bf16[1,1,1536]{2,1,0:T(2,128)(2,1)S(1)}, u32[]{:S(2)}, u32[]{:S(2)}) collective-permute-start(bf16[1,1,1536]{2,1,0:T(2,128)(2,1)S(1)} %collective-permute-done.14), channel_id=1, source_target_pairs={{0,30},{2,0},{4,2},{6,4},{8,6},{10,8},{12,10},{14,12},{16,14},{18,... | collective-permute-start | bytes 9224 | tf_op jit(solution)/shard_map/ppermute | solution.py:14
  92.9 1.2 collective-permute-done.15
  94.1 4.4 %collective-permute-start.16 = (bf16[1,1,1536]{2,1,0:T(2,128)(2,1)S(1)}, bf16[1,1,1536]{2,1,0:T(2,128)(2,1)S(1)}, u32[]{:S(2)}, u32[]{:S(2)}) collective-permute-start(bf16[1,1,1536]{2,1,0:T(2,128)(2,1)S(1)} %collective-permute-done.15), channel_id=1, source_target_pairs={{0,30},{2,0},{4,2},{6,4},{8,6},{10,8},{12,10},{14,12},{16,14},{18,... | collective-permute-start | bytes 9224 | tf_op jit(solution)/shard_map/ppermute | solution.py:14
  98.7 1.2 collective-permute-done.16
  99.9 4.4 %collective-permute-start.17 = (bf16[1,1,1536]{2,1,0:T(2,128)(2,1)S(1)}, bf16[1,1,1536]{2,1,0:T(2,128)(2,1)S(1)}, u32[]{:S(2)}, u32[]{:S(2)}) collective-permute-start(bf16[1,1,1536]{2,1,0:T(2,128)(2,1)S(1)} %collective-permute-done.16), channel_id=1, source_target_pairs={{0,30},{2,0},{4,2},{6,4},{8,6},{10,8},{12,10},{14,12},{16,14},{18,... | collective-permute-start | bytes 9224 | tf_op jit(solution)/shard_map/ppermute | solution.py:14
  104.4 1.2 collective-permute-done.17
  105.6 4.4 %collective-permute-start.18 = (bf16[1,1,1536]{2,1,0:T(2,128)(2,1)S(1)}, bf16[1,1,1536]{2,1,0:T(2,128)(2,1)S(1)}, u32[]{:S(2)}, u32[]{:S(2)}) collective-permute-start(bf16[1,1,1536]{2,1,0:T(2,128)(2,1)S(1)} %collective-permute-done.17), channel_id=1, source_target_pairs={{0,30},{2,0},{4,2},{6,4},{8,6},{10,8},{12,10},{14,12},{16,14},{18,... | collective-permute-start | bytes 9224 | tf_op jit(solution)/shard_map/ppermute | solution.py:14
  110.2 1.2 collective-permute-done.18
  111.4 1.1 fusion.17
  112.6 9.8 %all-reduce.1 = f32[1,2,1536]{2,1,0:T(2,128)S(1)} all-reduce(f32[1,2,1536]{2,1,0:T(2,128)S(1)} %copy.83), channel_id=2, replica_groups=mesh['gx'=16,'gy'=2] {'gy'}, use_global_device_ids=true, to_apply=%region_1.2.clone | all-reduce | flops 3072 | bytes 24576
  122.4 1.9 %fusion.61 = (f32[1,1,1536]{2,1,0:T(1,128)}, f32[1536]{0:T(1024)S(1)}) fusion(f32[1,2,1536]{2,1,0:T(2,128)S(1)} %all-reduce.1, u32[]{:T(128)} %bitcast.77, f32[1,1,1536]{2,1,0:T(1,128)} %param.18, f32[1536]{0:T(1024)S(1)} %gather_fusion, f32[1,1,1536]{2,1,0:T(1,128)} %param.17, f32[1,1,1536]{2,1,0:T(1,128)S(1)} %copy-done.17), kind=kLoop, calls=%fused_computation.130 | loop fusion | flops 7680 | bytes 43012 | tf_op jit(solution)/shard_map/add | solution.py:102
  124.2 6.2 %scatter_custom_fusion = f32[1536]{0:T(1024)S(1)} fusion(s32[1536]{0:T(1024)S(1)} %fusion.43, f32[1536]{0:T(1024)S(1)} %get-tuple-element.62, f32[]{:T(128)} %constant.143.clone.1), kind=kCustom, calls=%fused_computation.148 | custom fusion | bytes 6148 | tf_op jit(solution)/shard_map/scatter | solution.py:81
  131.2 1.1 pad_maximum_fusion
  132.4 1.1 fusion.26
  134.5 2.1 %copy.62 = f32[3,16,16,128]{2,1,0,3:T(8,128)S(1)} copy(f32[3,16,16,128]{3,2,1,0:T(8,128)} %pad_maximum_fusion.1) | data formatting | bytes 786432 | tf_op jit(solution)/shard_map/stack | solution.py:48
  136.6 1.8 %copy.81 = f32[3,16,16,128]{3,2,1,0:T(8,128)} copy(f32[3,16,16,128]{2,1,0,3:T(8,128)S(1)} %fusion.41) | data formatting | bytes 786432
  (80 shorter events, 8.1 us)
Async XLA Ops:
  0.6 110.8 %copy-start = (bf16[16,1,2,1536]{3,2,1,0:T(2,128)(2,1)S(1)}, bf16[16,1,2,1536]{3,2,1,0:T(2,128)(2,1)}, u32[]{:S(2)}) copy-start(bf16[16,1,2,1536]{3,2,1,0:T(2,128)(2,1)} %param.20) | copy-start | bytes 294916
  0.6 12.3 %copy-start.2 = (bf16[16,16,1,1536]{3,1,2,0:T(8,128)(2,1)S(1)}, bf16[16,16,1,1536]{3,1,2,0:T(8,128)(2,1)}, u32[]{:S(2)}) copy-start(bf16[16,16,1,1536]{3,1,2,0:T(8,128)(2,1)} %param.21) | copy-start | bytes 2359300
  1.4 24.3 %collective-permute-start.4 = (bf16[1,1,1536]{2,1,0:T(2,128)(2,1)S(1)}, bf16[1,1,1536]{2,1,0:T(2,128)(2,1)}, u32[]{:S(2)}, u32[]{:S(2)}) collective-permute-start(bf16[1,1,1536]{2,1,0:T(2,128)(2,1)S(1)} %convert_element_type.8), channel_id=1, source_target_pairs={{0,30},{2,0},{4,2},{6,4},{8,6},{10,8},{12,10},{14,12},{16,14},{18,... | collective-permute-start | bytes 9224 | tf_op jit(solution)/shard_map/ppermute | solution.py:14
  8.3 55.5 %collective-permute-start = (f32[3,1,16,128]{3,2,1,0:T(8,128)}, f32[3,1,16,128]{3,2,1,0:T(8,128)}, u32[]{:S(2)}, u32[]{:S(2)}) collective-permute-start(f32[3,1,16,128]{3,2,1,0:T(8,128)} %get-tuple-element.56), channel_id=1, source_target_pairs={{0,2},{2,4},{4,6},{6,8},{8,10},{10,12},{12,14},{14,16},{16,18},{18... | collective-permute-start | bytes 73736 | tf_op jit(solution)/shard_map/ppermute | solution.py:26
  10.2 55.8 %collective-permute-start.1 = (f32[3,1,16,128]{3,2,1,0:T(8,128)}, f32[3,1,16,128]{3,2,1,0:T(8,128)}, u32[]{:S(2)}, u32[]{:S(2)}) collective-permute-start(f32[3,1,16,128]{3,2,1,0:T(8,128)} %get-tuple-element.55), channel_id=1, source_target_pairs={{2,0},{4,2},{6,4},{8,6},{10,8},{12,10},{14,12},{16,14},{18,16},{20... | collective-permute-start | bytes 73736 | tf_op jit(solution)/shard_map/ppermute | solution.py:27
  13.0 2.7 %copy-start.16 = (f32[1,1,1536]{2,1,0:T(1,128)S(1)}, f32[1,1,1536]{2,1,0:T(1,128)}, u32[]{:S(2)}) copy-start(f32[1,1,1536]{2,1,0:T(1,128)} %param.16) | copy-start | bytes 18436
  13.0 3.5 %copy-start.18 = (s32[1,1,1536]{2,1,0:T(1,128)S(1)}, s32[1,1,1536]{2,1,0:T(1,128)}, u32[]{:S(2)}) copy-start(s32[1,1,1536]{2,1,0:T(1,128)} %param.19) | copy-start | bytes 18436
  13.0 3.6 %copy-start.1 = (f32[3,16,16,128]{3,2,1,0:T(8,128)S(1)}, f32[3,16,16,128]{3,2,1,0:T(8,128)}, u32[]{:S(2)}) copy-start(f32[3,16,16,128]{3,2,1,0:T(8,128)} %param.13) | copy-start | bytes 1179652
  16.8 8.4 %copy-start.19 = (u32[32]{0:T(128)S(1)}, u32[32]{0:T(128)}, u32[]{:S(2)}) copy-start(u32[32]{0:T(128)} %constant.175) | copy-start | bytes 388
  16.8 57.9 %copy-start.4 = (f32[3,3,16,16,128]{4,3,2,1,0:T(8,128)S(1)}, f32[3,3,16,16,128]{4,3,2,1,0:T(8,128)}, u32[]{:S(2)}) copy-start(f32[3,3,16,16,128]{4,3,2,1,0:T(8,128)} %param.14) | copy-start | bytes 3538948
  25.2 49.5 %copy-start.3 = (f32[6,2,16,16,128]{4,3,2,1,0:T(8,128)S(1)}, f32[6,2,16,16,128]{4,3,2,1,0:T(8,128)}, u32[]{:S(2)}) copy-start(f32[6,2,16,16,128]{4,3,2,1,0:T(8,128)} %param.15) | copy-start | bytes 4718596
  25.8 3.8 %collective-permute-start.5 = (bf16[1,1,1536]{2,1,0:T(2,128)(2,1)}, bf16[1,1,1536]{2,1,0:T(2,128)(2,1)S(1)}, u32[]{:S(2)}, u32[]{:S(2)}) collective-permute-start(bf16[1,1,1536]{2,1,0:T(2,128)(2,1)} %collective-permute-done.4), channel_id=1, source_target_pairs={{0,30},{2,0},{4,2},{6,4},{8,6},{10,8},{12,10},{14,12},{16,14},{18,... | collective-permute-start | bytes 9224 | tf_op jit(solution)/shard_map/ppermute | solution.py:14
  29.5 5.8 %collective-permute-start.6 = (bf16[1,1,1536]{2,1,0:T(2,128)(2,1)S(1)}, bf16[1,1,1536]{2,1,0:T(2,128)(2,1)S(1)}, u32[]{:S(2)}, u32[]{:S(2)}) collective-permute-start(bf16[1,1,1536]{2,1,0:T(2,128)(2,1)S(1)} %collective-permute-done.5), channel_id=1, source_target_pairs={{0,30},{2,0},{4,2},{6,4},{8,6},{10,8},{12,10},{14,12},{16,14},{18,... | collective-permute-start | bytes 9224 | tf_op jit(solution)/shard_map/ppermute | solution.py:14
  35.3 5.8 %collective-permute-start.7 = (bf16[1,1,1536]{2,1,0:T(2,128)(2,1)S(1)}, bf16[1,1,1536]{2,1,0:T(2,128)(2,1)S(1)}, u32[]{:S(2)}, u32[]{:S(2)}) collective-permute-start(bf16[1,1,1536]{2,1,0:T(2,128)(2,1)S(1)} %collective-permute-done.6), channel_id=1, source_target_pairs={{0,30},{2,0},{4,2},{6,4},{8,6},{10,8},{12,10},{14,12},{16,14},{18,... | collective-permute-start | bytes 9224 | tf_op jit(solution)/shard_map/ppermute | solution.py:14
  41.1 5.8 %collective-permute-start.8 = (bf16[1,1,1536]{2,1,0:T(2,128)(2,1)S(1)}, bf16[1,1,1536]{2,1,0:T(2,128)(2,1)S(1)}, u32[]{:S(2)}, u32[]{:S(2)}) collective-permute-start(bf16[1,1,1536]{2,1,0:T(2,128)(2,1)S(1)} %collective-permute-done.7), channel_id=1, source_target_pairs={{0,30},{2,0},{4,2},{6,4},{8,6},{10,8},{12,10},{14,12},{16,14},{18,... | collective-permute-start | bytes 9224 | tf_op jit(solution)/shard_map/ppermute | solution.py:14
  46.8 5.8 %collective-permute-start.9 = (bf16[1,1,1536]{2,1,0:T(2,128)(2,1)S(1)}, bf16[1,1,1536]{2,1,0:T(2,128)(2,1)S(1)}, u32[]{:S(2)}, u32[]{:S(2)}) collective-permute-start(bf16[1,1,1536]{2,1,0:T(2,128)(2,1)S(1)} %collective-permute-done.8), channel_id=1, source_target_pairs={{0,30},{2,0},{4,2},{6,4},{8,6},{10,8},{12,10},{14,12},{16,14},{18,... | collective-permute-start | bytes 9224 | tf_op jit(solution)/shard_map/ppermute | solution.py:14
  52.6 5.8 %collective-permute-start.10 = (bf16[1,1,1536]{2,1,0:T(2,128)(2,1)S(1)}, bf16[1,1,1536]{2,1,0:T(2,128)(2,1)S(1)}, u32[]{:S(2)}, u32[]{:S(2)}) collective-permute-start(bf16[1,1,1536]{2,1,0:T(2,128)(2,1)S(1)} %collective-permute-done.9), channel_id=1, source_target_pairs={{0,30},{2,0},{4,2},{6,4},{8,6},{10,8},{12,10},{14,12},{16,14},{18,... | collective-permute-start | bytes 9224 | tf_op jit(solution)/shard_map/ppermute | solution.py:14
  58.3 17.2 %collective-permute-start.11 = (bf16[1,1,1536]{2,1,0:T(2,128)(2,1)S(1)}, bf16[1,1,1536]{2,1,0:T(2,128)(2,1)S(1)}, u32[]{:S(2)}, u32[]{:S(2)}) collective-permute-start(bf16[1,1,1536]{2,1,0:T(2,128)(2,1)S(1)} %collective-permute-done.10), channel_id=1, source_target_pairs={{0,30},{2,0},{4,2},{6,4},{8,6},{10,8},{12,10},{14,12},{16,14},{18,... | collective-permute-start | bytes 9224 | tf_op jit(solution)/shard_map/ppermute | solution.py:14
  65.1 10.4 %copy-start.14 = (bf16[16,1,1,1536]{3,1,2,0:T(2,128)(2,1)S(1)}, bf16[16,1,1,1536]{3,1,2,0:T(2,128)(2,1)}, u32[]{:S(2)}) copy-start(bf16[16,1,1,1536]{3,1,2,0:T(2,128)(2,1)} %get-tuple-element.37) | copy-start | bytes 147460
  65.1 16.2 %copy-start.13 = (bf16[16,1,1,1536]{3,1,2,0:T(2,128)(2,1)S(1)}, bf16[16,1,1,1536]{3,1,2,0:T(2,128)(2,1)}, u32[]{:S(2)}) copy-start(bf16[16,1,1,1536]{3,1,2,0:T(2,128)(2,1)} %get-tuple-element.36) | copy-start | bytes 147460
  65.1 21.9 %copy-start.12 = (bf16[16,1,1,1536]{3,1,2,0:T(2,128)(2,1)S(1)}, bf16[16,1,1,1536]{3,1,2,0:T(2,128)(2,1)}, u32[]{:S(2)}) copy-start(bf16[16,1,1,1536]{3,1,2,0:T(2,128)(2,1)} %get-tuple-element.35) | copy-start | bytes 147460
  65.9 9.6 %copy-start.7 = (f32[3,17,16,128]{3,2,1,0:T(8,128)}, f32[3,17,16,128]{3,2,1,0:T(8,128)S(1)}, u32[]{:S(2)}) copy-start(f32[3,17,16,128]{3,2,1,0:T(8,128)S(1)} %get-tuple-element.54) | copy-start | bytes 1253380
  65.9 26.9 %copy-start.11 = (bf16[16,1,1,1536]{3,1,2,0:T(2,128)(2,1)S(1)}, bf16[16,1,1,1536]{3,1,2,0:T(2,128)(2,1)}, u32[]{:S(2)}) copy-start(bf16[16,1,1,1536]{3,1,2,0:T(2,128)(2,1)} %get-tuple-element.34) | copy-start | bytes 147460
  65.9 32.6 %copy-start.10 = (bf16[16,1,1,1536]{3,1,2,0:T(2,128)(2,1)S(1)}, bf16[16,1,1,1536]{3,1,2,0:T(2,128)(2,1)}, u32[]{:S(2)}) copy-start(bf16[16,1,1,1536]{3,1,2,0:T(2,128)(2,1)} %get-tuple-element.33) | copy-start | bytes 147460
  65.9 38.4 %copy-start.9 = (bf16[16,1,1,1536]{3,1,2,0:T(2,128)(2,1)S(1)}, bf16[16,1,1,1536]{3,1,2,0:T(2,128)(2,1)}, u32[]{:S(2)}) copy-start(bf16[16,1,1,1536]{3,1,2,0:T(2,128)(2,1)} %get-tuple-element.32) | copy-start | bytes 147460
  65.9 44.1 %copy-start.8 = (bf16[16,1,1,1536]{3,1,2,0:T(2,128)(2,1)S(1)}, bf16[16,1,1,1536]{3,1,2,0:T(2,128)(2,1)}, u32[]{:S(2)}) copy-start(bf16[16,1,1,1536]{3,1,2,0:T(2,128)(2,1)} %get-tuple-element.31) | copy-start | bytes 147460
  65.9 56.4 %copy-start.17 = (f32[1,1,1536]{2,1,0:T(1,128)S(1)}, f32[1,1,1536]{2,1,0:T(1,128)}, u32[]{:S(2)}) copy-start(f32[1,1,1536]{2,1,0:T(1,128)} %param.16) | copy-start | bytes 18436
  67.5 7.2 %copy-start.5 = (f32[3,17,16,128]{3,2,1,0:T(8,128)}, f32[3,17,16,128]{3,2,1,0:T(8,128)S(1)}, u32[]{:S(2)}) copy-start(f32[3,17,16,128]{3,2,1,0:T(8,128)S(1)} %get-tuple-element.57) | copy-start | bytes 1253380
  69.4 61.8 %collective-permute-start.2 = (f32[3,18,1,128]{3,2,1,0:T(1,128)}, f32[3,18,1,128]{3,2,1,0:T(1,128)}, u32[]{:S(2)}, u32[]{:S(2)}) collective-permute-start(f32[3,18,1,128]{3,2,1,0:T(1,128)} %get-tuple-element.48), channel_id=1, source_target_pairs={{0,1},{2,3},{4,5},{6,7},{8,9},{10,11},{12,13},{14,15},{16,17},{18,... | collective-permute-start | bytes 82952 | tf_op jit(solution)/shard_map/ppermute | solution.py:26
  73.4 57.8 %collective-permute-start.3 = (f32[3,18,1,128]{3,2,1,0:T(1,128)}, f32[3,18,1,128]{3,2,1,0:T(1,128)}, u32[]{:S(2)}, u32[]{:S(2)}) collective-permute-start(f32[3,18,1,128]{3,2,1,0:T(1,128)} %get-tuple-element.49), channel_id=1, source_target_pairs={{1,0},{3,2},{5,4},{7,6},{9,8},{11,10},{13,12},{15,14},{17,16},{19,... | collective-permute-start | bytes 82952 | tf_op jit(solution)/shard_map/ppermute | solution.py:27
  75.5 1.4 collective-permute-start.12
  76.9 5.8 %collective-permute-start.13 = (bf16[1,1,1536]{2,1,0:T(2,128)(2,1)S(1)}, bf16[1,1,1536]{2,1,0:T(2,128)(2,1)S(1)}, u32[]{:S(2)}, u32[]{:S(2)}) collective-permute-start(bf16[1,1,1536]{2,1,0:T(2,128)(2,1)S(1)} %collective-permute-done.12), channel_id=1, source_target_pairs={{0,30},{2,0},{4,2},{6,4},{8,6},{10,8},{12,10},{14,12},{16,14},{18,... | collective-permute-start | bytes 9224 | tf_op jit(solution)/shard_map/ppermute | solution.py:14
  82.6 5.8 %collective-permute-start.14 = (bf16[1,1,1536]{2,1,0:T(2,128)(2,1)S(1)}, bf16[1,1,1536]{2,1,0:T(2,128)(2,1)S(1)}, u32[]{:S(2)}, u32[]{:S(2)}) collective-permute-start(bf16[1,1,1536]{2,1,0:T(2,128)(2,1)S(1)} %collective-permute-done.13), channel_id=1, source_target_pairs={{0,30},{2,0},{4,2},{6,4},{8,6},{10,8},{12,10},{14,12},{16,14},{18,... | collective-permute-start | bytes 9224 | tf_op jit(solution)/shard_map/ppermute | solution.py:14
  88.4 5.8 %collective-permute-start.15 = (bf16[1,1,1536]{2,1,0:T(2,128)(2,1)S(1)}, bf16[1,1,1536]{2,1,0:T(2,128)(2,1)S(1)}, u32[]{:S(2)}, u32[]{:S(2)}) collective-permute-start(bf16[1,1,1536]{2,1,0:T(2,128)(2,1)S(1)} %collective-permute-done.14), channel_id=1, source_target_pairs={{0,30},{2,0},{4,2},{6,4},{8,6},{10,8},{12,10},{14,12},{16,14},{18,... | collective-permute-start | bytes 9224 | tf_op jit(solution)/shard_map/ppermute | solution.py:14
  94.1 5.8 %collective-permute-start.16 = (bf16[1,1,1536]{2,1,0:T(2,128)(2,1)S(1)}, bf16[1,1,1536]{2,1,0:T(2,128)(2,1)S(1)}, u32[]{:S(2)}, u32[]{:S(2)}) collective-permute-start(bf16[1,1,1536]{2,1,0:T(2,128)(2,1)S(1)} %collective-permute-done.15), channel_id=1, source_target_pairs={{0,30},{2,0},{4,2},{6,4},{8,6},{10,8},{12,10},{14,12},{16,14},{18,... | collective-permute-start | bytes 9224 | tf_op jit(solution)/shard_map/ppermute | solution.py:14
  99.9 5.8 %collective-permute-start.17 = (bf16[1,1,1536]{2,1,0:T(2,128)(2,1)S(1)}, bf16[1,1,1536]{2,1,0:T(2,128)(2,1)S(1)}, u32[]{:S(2)}, u32[]{:S(2)}) collective-permute-start(bf16[1,1,1536]{2,1,0:T(2,128)(2,1)S(1)} %collective-permute-done.16), channel_id=1, source_target_pairs={{0,30},{2,0},{4,2},{6,4},{8,6},{10,8},{12,10},{14,12},{16,14},{18,... | collective-permute-start | bytes 9224 | tf_op jit(solution)/shard_map/ppermute | solution.py:14
  105.6 5.8 %collective-permute-start.18 = (bf16[1,1,1536]{2,1,0:T(2,128)(2,1)S(1)}, bf16[1,1,1536]{2,1,0:T(2,128)(2,1)S(1)}, u32[]{:S(2)}, u32[]{:S(2)}) collective-permute-start(bf16[1,1,1536]{2,1,0:T(2,128)(2,1)S(1)} %collective-permute-done.17), channel_id=1, source_target_pairs={{0,30},{2,0},{4,2},{6,4},{8,6},{10,8},{12,10},{14,12},{16,14},{18,... | collective-permute-start | bytes 9224 | tf_op jit(solution)/shard_map/ppermute | solution.py:14
  132.4 1.3 copy-start.6
  134.5 2.1 %copy-start.15 = (f32[3,16,16,1]{2,1,0,3:T(8,128)S(1)}, f32[3,16,16,1]{2,1,0,3:T(8,128)}, u32[]{:S(2)}) copy-start(f32[3,16,16,1]{2,1,0,3:T(8,128)} %reshape.261) | copy-start | bytes 9220
